TPU v7x, 32 devices: a whole 2x2x4 slice. The times are simulated.
32 devices in a mesh: blk: 4 (over y, x), dp: 8 (over z, core).
Axes of the slice: x: 2, y: 2, z: 4, core: 2. Of those that a mesh axis runs over, the one named last changes fastest.
Arguments:
- patches: bfloat16 [4096, 64, 256], P(('blk', 'dp')), may hold values from -6 to 6
- w_mix: bfloat16 [256, 128], replicated, may hold values from -0.375 to 0.375
- w_in: bfloat16 [2048, 512], replicated, may hold values from -0.125 to 0.125
- w_out: bfloat16 [512, 128], replicated, may hold values from -0.25 to 0.25
- partner_dev: int32 [4096], P(('blk', 'dp')), may hold values from 0 to 7, as said below
- partner_row: int32 [4096], P(('blk', 'dp')), may hold values from 0 to 127, as said below
Outputs:
- loss_rows: float32 [4096], P(('blk', 'dp'))
- grad_mix: float32 [256, 128], replicated
- grad_in: float32 [2048, 512], replicated
- grad_out: float32 [512, 128], replicated
Inputs may be any that keep to these rules, and one draw needn't show every extreme that they name: Among one device's rows every dp index appears as partner_dev exactly 128/8 times. Over the rows that share a blk index, the pairs (partner_dev, partner_row) name every pair of dp index and row of a device exactly once.
All inputs are finite; a program needn't handle non-finite values.
Results may differ from a plain program's by a relative error of at most 0.012.
The roundings to bfloat16 on the way count: a program that leaves them out, or rounds other values in their place, can miss the bound.
Values may be sent and summed in bfloat16 or wider, within the bound.
No kernel may reach another device: no remote copies, remote signals or barrier semaphores. Data moves between devices by JAX's collectives and lax.ppermute only.
A program may use at most 64 MiB of HBM per device.

v0:
```python
import math
import jax
import jax.numpy as jnp
from jax import lax
from jax.sharding import PartitionSpec as P

SCALE = 10.0


def dft_table(length, freqs):
    angle_idx = jnp.arange(length, dtype=jnp.int32)
    freq_idx = jnp.arange(freqs, dtype=jnp.int32)
    phase = jnp.mod(freq_idx[None, :] * angle_idx[:, None], length).astype(jnp.float32) * (
        2.0 * math.pi / length
    )
    return jnp.concatenate([jnp.cos(phase), -jnp.sin(phase)], axis=1).astype(jnp.bfloat16)


def encode(block, w_mix, w_in, w_out):
    count, length, lanes = block.shape
    filters = w_mix.shape[1]
    freqs = w_in.shape[0] // filters
    angle_table = dft_table(length, freqs)
    spec = jnp.einsum("pac,ak->pkc", block, angle_table, preferred_element_type=jnp.float32).astype(
        jnp.bfloat16
    )
    mixed = jnp.dot(spec.reshape(-1, lanes), w_mix, preferred_element_type=jnp.float32).reshape(
        count, 2 * freqs, filters
    )
    real_part = mixed[:, :freqs]
    imag_part = mixed[:, freqs:]
    powers = real_part * real_part + imag_part * imag_part
    features = jnp.log1p(powers).reshape(count, -1)
    mean_removed = features - jnp.mean(features, axis=1, keepdims=True)
    reciprocal_scale = lax.rsqrt(
        jnp.mean(mean_removed * mean_removed, axis=1, keepdims=True) + 1e-05
    )
    normed = (mean_removed * reciprocal_scale).astype(jnp.bfloat16)
    preact = jnp.dot(normed, w_in, preferred_element_type=jnp.float32)
    hidden = jax.nn.silu(preact).astype(jnp.bfloat16)
    raw_embed = jnp.dot(hidden, w_out, preferred_element_type=jnp.float32)
    norms = jnp.sqrt(jnp.sum(raw_embed * raw_embed, axis=1, keepdims=True) + 1e-06)
    unit32 = raw_embed / norms
    saved = (
        spec,
        real_part,
        imag_part,
        powers,
        mean_removed,
        reciprocal_scale,
        normed,
        preact,
        hidden,
        unit32,
        norms,
    )
    return (unit32.astype(jnp.bfloat16), saved)


def back_upper(grad_units, saved, w_in, w_out):
    (
        spec,
        real_part,
        imag_part,
        powers,
        mean_removed,
        reciprocal_scale,
        normed,
        preact,
        hidden,
        unit32,
        norms,
    ) = saved
    grad_raw = (
        (grad_units - unit32 * jnp.sum(unit32 * grad_units, axis=1, keepdims=True)) / norms
    ).astype(jnp.bfloat16)
    g_out = jnp.dot(hidden.T, grad_raw, preferred_element_type=jnp.float32)
    grad_hid = jnp.dot(grad_raw, w_out.T, preferred_element_type=jnp.float32)
    sigm = jax.nn.sigmoid(preact)
    grad_pre = (grad_hid * sigm * (1.0 + preact * (1.0 - sigm))).astype(jnp.bfloat16)
    g_in = jnp.dot(normed.T, grad_pre, preferred_element_type=jnp.float32)
    norm_gradient = jnp.dot(grad_pre, w_in.T, preferred_element_type=jnp.float32)
    return (g_in, g_out, norm_gradient)


def back_lower(norm_gradient, saved):
    (
        spec,
        real_part,
        imag_part,
        powers,
        mean_removed,
        reciprocal_scale,
        normed,
        preact,
        hidden,
        unit32,
        norms,
    ) = saved
    lanes = spec.shape[2]
    normalized_input = mean_removed * reciprocal_scale
    feature_gradient = reciprocal_scale * (
        norm_gradient
        - jnp.mean(norm_gradient, axis=1, keepdims=True)
        - normalized_input * jnp.mean(norm_gradient * normalized_input, axis=1, keepdims=True)
    )
    grad_pow = feature_gradient.reshape(powers.shape) / (1.0 + powers)
    grad_mixed = jnp.concatenate(
        [2.0 * real_part * grad_pow, 2.0 * imag_part * grad_pow], axis=1
    ).astype(jnp.bfloat16)
    return jnp.dot(
        spec.reshape(-1, lanes).T,
        grad_mixed.reshape(-1, grad_mixed.shape[2]),
        preferred_element_type=jnp.float32,
    )


def negative_part(units, piece, row_ids):
    scores = SCALE * jnp.dot(units, piece.T, preferred_element_type=jnp.float32)
    column = jnp.arange(piece.shape[0], dtype=jnp.int32)
    expo = jnp.where(column[None, :] == row_ids[:, None], jnp.float32(0.0), jnp.exp(scores))
    return (
        jnp.sum(expo, axis=1),
        jnp.dot(expo.astype(jnp.bfloat16), piece, preferred_element_type=jnp.float32),
    )


def key_part(units, piece, tot_piece, row_ids):
    scores = SCALE * jnp.dot(piece, units.T, preferred_element_type=jnp.float32)
    column = jnp.arange(piece.shape[0], dtype=jnp.int32)
    expo = jnp.where(column[:, None] == row_ids[None, :], jnp.float32(0.0), jnp.exp(scores))
    weights = (expo / tot_piece[:, None]).astype(jnp.bfloat16)
    return jnp.dot(weights.T, piece, preferred_element_type=jnp.float32)


def on_device(patches, w_mix, w_in, w_out, partner_dev, partner_row):
    count = patches.shape[0]
    embed = w_out.shape[1]
    units, saved = encode(patches, w_mix, w_in, w_out)
    peers = lax.axis_size("dp")
    per_peer = count // peers
    sorted_positions = jnp.argsort(partner_dev, stable=True)
    inverse = jnp.argsort(sorted_positions, stable=True)
    wanted = partner_row[sorted_positions].reshape(peers, per_peer)
    asked = lax.all_to_all(wanted, "dp", split_axis=0, concat_axis=0, tiled=True)
    picked = units[asked]
    returned_rows = lax.all_to_all(picked, "dp", split_axis=0, concat_axis=0, tiled=True)
    positive = returned_rows.reshape(count, embed)[inverse]
    spos = SCALE * jnp.sum(units.astype(jnp.float32) * positive.astype(jnp.float32), axis=1)
    row_ids = lax.axis_index("blk") * count + jnp.arange(count, dtype=jnp.int32)
    zpart, npart = negative_part(units, lax.all_gather(units, "blk", axis=0, tiled=True), row_ids)
    totals = jnp.exp(spos) + zpart
    all_totals = lax.all_gather(totals, "blk", axis=0, tiled=True)
    keyterm = key_part(units, lax.all_gather(units, "blk", axis=0, tiled=True), all_totals, row_ids)
    loss_rows = jnp.log(totals) - spos
    coef = SCALE / count
    ppos = jnp.exp(spos) / totals
    partner_grad = coef * (ppos - 1.0)[:, None] * units.astype(jnp.float32)
    outgoing = partner_grad[sorted_positions].reshape(peers, per_peer, embed)
    incoming = lax.all_to_all(outgoing, "dp", split_axis=0, concat_axis=0, tiled=True)
    from_partner = (
        jnp.zeros((count, embed), jnp.float32)
        .at[asked.reshape(-1)]
        .add(incoming.reshape(-1, embed))
    )
    grad_units = (
        coef * ((ppos - 1.0)[:, None] * positive.astype(jnp.float32) + npart / totals[:, None])
        + coef * keyterm
        + from_partner
    )
    g_in, g_out, norm_gradient = back_upper(grad_units, saved, w_in, w_out)
    g_mix = back_lower(norm_gradient, saved)
    g_mix, g_in, g_out = lax.psum((g_mix, g_in, g_out), ("blk", "dp"))
    return (loss_rows, g_mix, g_in, g_out)


def solution(mesh):
    placed = (P(("blk", "dp"), None, None), P(), P(), P(), P(("blk", "dp")), P(("blk", "dp")))
    return jax.shard_map(
        on_device,
        mesh=mesh,
        in_specs=placed,
        out_specs=(P(("blk", "dp")), P(), P(), P()),
        check_vma=False,
    )
```

profile of v0, /device:TPU:0, one launch (start us, length us, event | category | flops | bytes accessed | tf_op | source)
XLA Modules:
  0.0 252.2 jit_solution(4154058484988354202)
XLA Ops:
  7.2 3.3 %sort.31 = (s32[128]{0:T(128)}, s32[128]{0:T(128)S(1)}) sort(s32[128]{0:T(128)} %param.10, s32[128]{0:T(128)S(1)} %iota.30), dimensions={0}, to_apply=%region_3.4 | sort | flops 896 | bytes 2048 | tf_op jit(solution)/shard_map/jit(argsort)/sort | solution.py:142
  10.5 1.6 gather_fusion
  12.8 6.4 %all-to-all-start = ((s32[8,1,16]{2,1,0:T(1,128)}), s32[8,1,16]{2,1,0:T(1,128)S(1)}, u32[]{:S(2)}, u32[]{:S(2)}) async-start(s32[8,1,16]{2,1,0:T(1,128)} %bitcast.4), calls=%async_computation | async-start | bytes 8192 | tf_op jit(solution)/shard_map/all_to_all | solution.py:145
  19.3 2.5 %sort.32 = (s32[128]{0:T(128)}, s32[128]{0:T(128)S(1)}) sort(s32[128]{0:T(128)S(1)} %get-tuple-element.6, s32[128]{0:T(128)S(1)} %iota.31), dimensions={0}, to_apply=%region_4.5 | sort | flops 896 | bytes 2048 | tf_op jit(solution)/shard_map/jit(argsort)/sort | solution.py:143
  21.8 2.9 %convert_bitcast_fusion = bf16[128,32,256]{2,1,0:T(8,128)(2,1)S(1)} fusion(bf16[128,64,256]{2,1,0:T(8,128)(2,1)} %param.6, bf16[64,16]{0,1:T(8,128)(2,1)S(1)} %get-tuple-element.27, bf16[64,16]{0,1:T(8,128)(2,1)S(1)} %get-tuple-element.28), kind=kOutput, calls=%fused_computation.7 | convolution fusion | flops 135274496 | bytes 6295552 | tf_op jit(solution)/shard_map/pac,ak->pkc/dot_general | solution.py:24
  24.8 2.5 fusion
  28.9 1.6 copy.38
  30.5 1.2 multiply_convert_fusion.2
  32.0 8.5 %all_gather.7 = bf16[512,128]{0,1:T(8,128)(2,1)S(1)} all-gather(bf16[128,128]{0,1:T(8,128)(2,1)S(1)} %fusion.35), channel_id=1, replica_groups=mesh['blk'=4,'dp'=8] {'blk'}, dimensions={0}, use_global_device_ids=true | all-gather | bytes 163840 | tf_op jit(solution)/shard_map/all_gather | solution.py:151
  42.9 1.3 gather_fusion.1
  44.2 5.1 %all-to-all-start.1 = ((bf16[8,16,128]{2,1,0:T(8,128)(2,1)}), bf16[8,16,128]{2,1,0:T(8,128)(2,1)S(1)}, u32[]{:S(2)}, u32[]{:S(2)}) async-start(bf16[8,16,128]{2,1,0:T(8,128)(2,1)} %bitcast.6), calls=%async_computation.1 | async-start | bytes 65536 | tf_op jit(solution)/shard_map/all_to_all | solution.py:147
  49.9 5.2 %all-to-all-done.1 = bf16[8,16,128]{2,1,0:T(8,128)(2,1)S(1)} async-done(((bf16[8,16,128]{2,1,0:T(8,128)(2,1)}), bf16[8,16,128]{2,1,0:T(8,128)(2,1)S(1)}, u32[]{:S(2)}, u32[]{:S(2)}) %all-to-all-start.1) | async-done | bytes 32800 | tf_op jit(solution)/shard_map/all_to_all | solution.py:147
  56.4 8.5 %all-gather = f32[4,1,128]{2,1,0:T(1,128)} all-gather(f32[1,1,128]{2,1,0:T(1,128)S(1)} %bitcast.47), channel_id=1, replica_groups=mesh['blk'=4,'dp'=8] {'blk'}, dimensions={0}, use_global_device_ids=true | all-gather | bytes 2560 | tf_op jit(solution)/shard_map/all_gather | solution.py:153
  65.1 1.2 gather_fusion.3
  66.3 3.5 %all-to-all-start.2 = ((f32[8,16,128]{2,1,0:T(8,128)}), f32[8,16,128]{2,1,0:T(8,128)S(1)}, u32[]{:S(2)}, u32[]{:S(2)}) async-start(f32[8,16,128]{2,1,0:T(8,128)} %bitcast.11), calls=%async_computation.2 | async-start | bytes 131072 | tf_op jit(solution)/shard_map/all_to_all | solution.py:160
  69.9 1.2 fusion.13
  71.0 2.0 fusion.12
  73.1 0.9 copy.45
  74.0 1.7 all-to-all-done.2
  75.7 1.5 scatter_fusion
  77.3 1.8 fusion.44
  79.1 1.2 fusion.9
  80.3 0.9 fusion.40
  81.2 2.8 %fusion.36 = f32[2048,512]{1,0:T(8,128)} fusion(bf16[128,512]{1,0:T(8,128)(2,1)S(1)} %fusion.9, f32[128,2048]{1,0:T(8,128)S(1)} %copy.38, f32[128]{0:T(128)S(1)} %add_rsqrt_fusion, f32[128]{0:T(128)S(1)} %broadcast_multiply_fusion.4), kind=kOutput, calls=%fused_computation.91 | convolution fusion | flops 269221888 | bytes 5374976 | tf_op jit(solution)/shard_map/dot_general | solution.py:81
  84.1 1.4 subtract_multiply_fusion
  85.5 1.5 copy.48
  87.0 2.0 multiply_convert_fusion.1
  89.1 1.7 copy.49
  90.8 3.3 %convolution_bitcast_fusion = f32[256,128]{1,0:T(8,128)} fusion(bf16[128,32,256]{2,1,0:T(8,128)(2,1)} %copy-done.3, bf16[128,32,128]{2,1,0:T(8,128)(2,1)} %copy.49), kind=kOutput, calls=%fused_computation.19 | convolution fusion | flops 268435456 | bytes 3276800 | tf_op jit(solution)/shard_map/dot_general | solution.py:111
  95.3 143.1 %all-reduce.3.cloned.1.call-done = (f32[256,128]{1,0:T(8,128)}, f32[2048,512]{1,0:T(8,128)}, f32[512,128]{1,0:T(8,128)}) async-done(((f32[256,128]{1,0:T(8,128)}, f32[2048,512]{1,0:T(8,128)}, f32[512,128]{1,0:T(8,128)}), (f32[256,128]{1,0:T(8,128)}, f32[2048,512]{1,0:T(8,128)}, f32[512,128]{1,0:T(8,128)})) %all-reduce.3.cloned.1.call-update) | async-done | bytes 4587536 | tf_op jit(solution)/shard_map/psum | solution.py:173
  238.4 1.6 copy.60
  239.9 4.7 %copy.61 = f32[2048,512]{1,0:T(8,128)} copy(f32[2048,512]{1,0:T(8,128)} %get-tuple-element.33) | data formatting | bytes 8388608
  (71 shorter events, 9.3 us)
Async XLA Ops:
  7.2 23.3 %copy-start = (bf16[2048,512]{1,0:T(8,128)(2,1)S(1)}, bf16[2048,512]{1,0:T(8,128)(2,1)}, u32[]{:S(2)}) copy-start(bf16[2048,512]{1,0:T(8,128)(2,1)} %param.8) | copy-start | bytes 6291460
  12.8 28.7 %all-to-all-start = ((s32[8,1,16]{2,1,0:T(1,128)}), s32[8,1,16]{2,1,0:T(1,128)S(1)}, u32[]{:S(2)}, u32[]{:S(2)}) async-start(s32[8,1,16]{2,1,0:T(1,128)} %bitcast.4), calls=%async_computation | async-start | bytes 8192 | tf_op jit(solution)/shard_map/all_to_all | solution.py:145
  19.2 21.2 %copy-start.14 = (s32[128]{0:T(128)}, s32[128]{0:T(128)S(1)}, u32[]{:S(2)}) copy-start(s32[128]{0:T(128)S(1)} %iota_add_fusion) | copy-start | bytes 1540
  21.8 2.9 %copy-start.8 = (bf16[256,128]{1,0:T(8,128)(2,1)S(1)}, bf16[256,128]{1,0:T(8,128)(2,1)}, u32[]{:S(2)}) copy-start(bf16[256,128]{1,0:T(8,128)(2,1)} %param.7) | copy-start | bytes 196612
  24.7 2.5 %copy-start.3 = (bf16[128,32,256]{2,1,0:T(8,128)(2,1)}, bf16[128,32,256]{2,1,0:T(8,128)(2,1)S(1)}, u32[]{:S(2)}) copy-start(bf16[128,32,256]{2,1,0:T(8,128)(2,1)S(1)} %convert_bitcast_fusion) | copy-start | bytes 6291460
  27.3 1.3 copy-start.1
  27.8 1.2 copy-start.2
  30.5 1.2 copy-start.5
  31.7 9.7 %copy-start.6 = (bf16[128,512]{1,0:T(8,128)(2,1)}, bf16[128,512]{1,0:T(8,128)(2,1)S(1)}, u32[]{:S(2)}) copy-start(bf16[128,512]{1,0:T(8,128)(2,1)S(1)} %get-tuple-element.20) | copy-start | bytes 393220
  40.5 0.9 copy-start.7
  44.2 10.8 %all-to-all-start.1 = ((bf16[8,16,128]{2,1,0:T(8,128)(2,1)}), bf16[8,16,128]{2,1,0:T(8,128)(2,1)S(1)}, u32[]{:S(2)}, u32[]{:S(2)}) async-start(bf16[8,16,128]{2,1,0:T(8,128)(2,1)} %bitcast.6), calls=%async_computation.1 | async-start | bytes 65536 | tf_op jit(solution)/shard_map/all_to_all | solution.py:147
  55.9 9.1 %copy-start.9 = (f32[128]{0:T(128)}, f32[128]{0:T(128)S(1)}, u32[]{:S(2)}) copy-start(f32[128]{0:T(128)S(1)} %fusion.21) | copy-start | bytes 1540
  56.4 8.6 %copy-start.11 = (f32[128]{0:T(128)}, f32[128]{0:T(128)S(1)}, u32[]{:S(2)}) copy-start(f32[128]{0:T(128)S(1)} %get-tuple-element.15) | copy-start | bytes 1540
  66.3 9.3 %copy-start.13 = (s32[128]{0:T(128)S(1)}, s32[128]{0:T(128)}, u32[]{:S(2)}) copy-start(s32[128]{0:T(128)} %fusion.31) | copy-start | bytes 1540
  66.3 9.3 %all-to-all-start.2 = ((f32[8,16,128]{2,1,0:T(8,128)}), f32[8,16,128]{2,1,0:T(8,128)S(1)}, u32[]{:S(2)}, u32[]{:S(2)}) async-start(f32[8,16,128]{2,1,0:T(8,128)} %bitcast.11), calls=%async_computation.2 | async-start | bytes 131072 | tf_op jit(solution)/shard_map/all_to_all | solution.py:160
  69.8 168.5 %all-reduce.3.cloned.1.call-start = ((), (), s32[]{:S(2)}) async-start(), calls=%async_computation.3 | async-start | bytes 9175040 | tf_op jit(solution)/shard_map/psum | solution.py:173
  94.1 0.7 copy-start.10
  94.1 0.7 copy-start.12
  239.9 4.7 %copy-start.4 = (f32[512,128]{1,0:T(8,128)S(1)}, f32[512,128]{1,0:T(8,128)}, u32[]{:S(2)}) copy-start(f32[512,128]{1,0:T(8,128)} %get-tuple-element.34) | copy-start | bytes 786436
Sparse Core Ops, SparseCore 0:
  94.2 144.0 all-reduce.2
where the time goes:
time: 253 us; the launch traced here: 252 us
  waiting for transfers between devices  150 us (59%)
  matrix products  21 us (8%)
  local copies, waits for them, and re-layouts  20.8 us (8%)
  blocking collectives  17 us (7%)
  starting transfers between devices  15 us (6%)
  between operations  14.3 us (6%)
  other arithmetic  14.1 us (6%)
    psum x1, waiting for transfers between devices, on_device(): g_mix, g_in, g_out = lax.psum((g_mix, g_in, g_out), ('blk', 'dp'))  143 us
    all_gather x1, blocking collectives, on_device(): all_totals = lax.all_gather(totals, 'blk', axis=0, tiled=True)  8.55 us
    unnamed x33, local copies, waits for them, and re-layouts  8.52 us
    all_gather x1, blocking collectives, on_device(): lax.all_gather(units, 'blk', axis=0, tiled=True)  8.46 us
    all_to_all x1, starting transfers between devices, on_device(): lax.all_to_all(wanted, 'dp', split_axis=0, concat_axis=0, tiled=True)  6.35 us
    all_to_all x1, waiting for transfers between devices, on_device(): lax.all_to_all(picked, 'dp', split_axis=0, concat_axis=0, tiled=True)  5.16 us
    all_to_all x1, starting transfers between devices, on_device(): lax.all_to_all(picked, 'dp', split_axis=0, concat_axis=0, tiled=True)  5.09 us
  transfers between devices with their start and end apart: 4, of which 3 were waited for; matrix products, arithmetic and copies ran while one was open for 7% of the time, Pallas kernels for 0%

commit v1 on v0

--- a/solution.py
+++ b/solution.py
@@ -170,7 +170,7 @@
     )
     g_in, g_out, norm_gradient = back_upper(grad_units, saved, w_in, w_out)
     g_mix = back_lower(norm_gradient, saved)
-    g_mix, g_in, g_out = lax.psum((g_mix, g_in, g_out), ("blk", "dp"))
+    g_mix, g_in, g_out = lax.psum(lax.psum((g_mix, g_in, g_out), "dp"), "blk")
     return (loss_rows, g_mix, g_in, g_out)
 
 

time: 253 us -> 325 us (1.28)
  waiting for transfers between devices: 150 us -> 223 us
    psum x1 -> x2, waiting for transfers between devices: 143 us -> 216 us  [on_device(): g_mix, g_in, g_out = lax.psum(lax.psum((g_mix, g_in, g_out), 'dp'), 'blk')]
  transfers between devices with their start and end apart: 4 -> 5, of which waited for: 3 -> 4; matrix products, arithmetic and copies ran while one was open for 7% -> 6% of each run, Pallas kernels for 0% -> 0%
where the time goes in v1:
time: 325 us
  waiting for transfers between devices  223 us (69%)
  matrix products  21 us (6%)
  local copies, waits for them, and re-layouts  20.8 us (6%)
  blocking collectives  17 us (5%)
  starting transfers between devices  15 us (5%)
  between operations  14.3 us (4%)
  other arithmetic  14.1 us (4%)
    psum x2, waiting for transfers between devices, on_device(): g_mix, g_in, g_out = lax.psum(lax.psum((g_mix, g_in, g_out), 'dp'), 'blk')  216 us
    all_gather x1, blocking collectives, on_device(): all_totals = lax.all_gather(totals, 'blk', axis=0, tiled=True)  8.54 us
    unnamed x33, local copies, waits for them, and re-layouts  8.49 us
    all_gather x1, blocking collectives, on_device(): lax.all_gather(units, 'blk', axis=0, tiled=True)  8.46 us
  transfers between devices with their start and end apart: 5, of which 4 were waited for; matrix products, arithmetic and copies ran while one was open for 6% of the time, Pallas kernels for 0%

profile of v1, /device:TPU:0, one launch (start us, length us, event | category | flops | bytes accessed | tf_op | source)
XLA Modules:
  0.0 324.8 jit_solution(1809138240115954826)
XLA Ops:
  7.2 3.3 %sort.31 = (s32[128]{0:T(128)}, s32[128]{0:T(128)S(1)}) sort(s32[128]{0:T(128)} %param.10, s32[128]{0:T(128)S(1)} %iota.30), dimensions={0}, to_apply=%region_3.4 | sort | flops 896 | bytes 2048 | tf_op jit(solution)/shard_map/jit(argsort)/sort | solution.py:142
  10.5 1.6 gather_fusion
  12.8 6.4 %all-to-all-start = ((s32[8,1,16]{2,1,0:T(1,128)}), s32[8,1,16]{2,1,0:T(1,128)S(1)}, u32[]{:S(2)}, u32[]{:S(2)}) async-start(s32[8,1,16]{2,1,0:T(1,128)} %bitcast.4), calls=%async_computation | async-start | bytes 8192 | tf_op jit(solution)/shard_map/all_to_all | solution.py:145
  19.3 2.5 sort.32
  21.8 2.9 convert_bitcast_fusion
  24.8 2.5 fusion
  28.9 1.6 copy.38
  30.5 1.2 multiply_convert_fusion.2
  32.0 8.5 %all_gather.7 = bf16[512,128]{0,1:T(8,128)(2,1)S(1)} all-gather(bf16[128,128]{0,1:T(8,128)(2,1)S(1)} %fusion.35), channel_id=1, replica_groups=mesh['blk'=4,'dp'=8] {'blk'}, dimensions={0}, use_global_device_ids=true | all-gather | bytes 163840 | tf_op jit(solution)/shard_map/all_gather | solution.py:151
  42.9 1.3 gather_fusion.1
  44.2 5.1 %all-to-all-start.1 = ((bf16[8,16,128]{2,1,0:T(8,128)(2,1)}), bf16[8,16,128]{2,1,0:T(8,128)(2,1)S(1)}, u32[]{:S(2)}, u32[]{:S(2)}) async-start(bf16[8,16,128]{2,1,0:T(8,128)(2,1)} %bitcast.6), calls=%async_computation.1 | async-start | bytes 65536 | tf_op jit(solution)/shard_map/all_to_all | solution.py:147
  49.9 5.2 %all-to-all-done.1 = bf16[8,16,128]{2,1,0:T(8,128)(2,1)S(1)} async-done(((bf16[8,16,128]{2,1,0:T(8,128)(2,1)}), bf16[8,16,128]{2,1,0:T(8,128)(2,1)S(1)}, u32[]{:S(2)}, u32[]{:S(2)}) %all-to-all-start.1) | async-done | bytes 32800 | tf_op jit(solution)/shard_map/all_to_all | solution.py:147
  56.4 8.5 %all-gather = f32[4,1,128]{2,1,0:T(1,128)} all-gather(f32[1,1,128]{2,1,0:T(1,128)S(1)} %bitcast.47), channel_id=1, replica_groups=mesh['blk'=4,'dp'=8] {'blk'}, dimensions={0}, use_global_device_ids=true | all-gather | bytes 2560 | tf_op jit(solution)/shard_map/all_gather | solution.py:153
  65.1 1.2 gather_fusion.3
  66.3 3.5 %all-to-all-start.2 = ((f32[8,16,128]{2,1,0:T(8,128)}), f32[8,16,128]{2,1,0:T(8,128)S(1)}, u32[]{:S(2)}, u32[]{:S(2)}) async-start(f32[8,16,128]{2,1,0:T(8,128)} %bitcast.11), calls=%async_computation.2 | async-start | bytes 131072 | tf_op jit(solution)/shard_map/all_to_all | solution.py:160
  69.9 1.2 fusion.13
  71.0 2.0 fusion.12
  73.1 0.9 copy.45
  74.0 1.7 all-to-all-done.2
  75.7 1.5 scatter_fusion
  77.3 1.8 fusion.44
  79.1 1.2 fusion.9
  81.2 2.8 fusion.36
  84.1 1.4 subtract_multiply_fusion
  85.5 1.5 copy.48
  87.1 2.0 multiply_convert_fusion.1
  89.1 1.7 copy.49
  90.8 3.3 %convolution_bitcast_fusion = f32[256,128]{1,0:T(8,128)} fusion(bf16[128,32,256]{2,1,0:T(8,128)(2,1)} %copy-done.3, bf16[128,32,128]{2,1,0:T(8,128)(2,1)} %copy.49), kind=kOutput, calls=%fused_computation.19 | convolution fusion | flops 268435456 | bytes 3276800 | tf_op jit(solution)/shard_map/dot_general | solution.py:111
  94.2 102.8 %all-reduce.5.cloned.1.call-done = (f32[256,128]{1,0:T(8,128)}, f32[2048,512]{1,0:T(8,128)}, f32[512,128]{1,0:T(8,128)}) async-done(((f32[256,128]{1,0:T(8,128)}, f32[2048,512]{1,0:T(8,128)}, f32[512,128]{1,0:T(8,128)}), (f32[256,128]{1,0:T(8,128)}, f32[2048,512]{1,0:T(8,128)}, f32[512,128]{1,0:T(8,128)})) %all-reduce.5.cloned.1.call-update) | async-done | bytes 4587536 | tf_op jit(solution)/shard_map/psum | solution.py:173
  198.1 112.9 %all-reduce.7.cloned.1.call-done = (f32[256,128]{1,0:T(8,128)}, f32[2048,512]{1,0:T(8,128)}, f32[512,128]{1,0:T(8,128)}) async-done(((f32[256,128]{1,0:T(8,128)}, f32[2048,512]{1,0:T(8,128)}, f32[512,128]{1,0:T(8,128)}), (f32[256,128]{1,0:T(8,128)}, f32[2048,512]{1,0:T(8,128)}, f32[512,128]{1,0:T(8,128)})) %all-reduce.7.cloned.1.call-update) | async-done | bytes 4587536 | tf_op jit(solution)/shard_map/psum | solution.py:173
  311.0 1.6 copy.63
  312.6 4.7 %copy.64 = f32[2048,512]{1,0:T(8,128)} copy(f32[2048,512]{1,0:T(8,128)} %get-tuple-element.36) | data formatting | bytes 8388608
  (74 shorter events, 10.3 us)
Async XLA Ops:
  7.2 23.3 %copy-start = (bf16[2048,512]{1,0:T(8,128)(2,1)S(1)}, bf16[2048,512]{1,0:T(8,128)(2,1)}, u32[]{:S(2)}) copy-start(bf16[2048,512]{1,0:T(8,128)(2,1)} %param.8) | copy-start | bytes 6291460
  12.8 28.7 %all-to-all-start = ((s32[8,1,16]{2,1,0:T(1,128)}), s32[8,1,16]{2,1,0:T(1,128)S(1)}, u32[]{:S(2)}, u32[]{:S(2)}) async-start(s32[8,1,16]{2,1,0:T(1,128)} %bitcast.4), calls=%async_computation | async-start | bytes 8192 | tf_op jit(solution)/shard_map/all_to_all | solution.py:145
  19.2 21.2 %copy-start.14 = (s32[128]{0:T(128)}, s32[128]{0:T(128)S(1)}, u32[]{:S(2)}) copy-start(s32[128]{0:T(128)S(1)} %iota_add_fusion) | copy-start | bytes 1540
  21.8 2.9 copy-start.8
  24.7 2.5 copy-start.3
  27.3 1.3 copy-start.1
  27.8 1.2 copy-start.2
  30.5 1.2 copy-start.5
  31.7 9.7 %copy-start.6 = (bf16[128,512]{1,0:T(8,128)(2,1)}, bf16[128,512]{1,0:T(8,128)(2,1)S(1)}, u32[]{:S(2)}) copy-start(bf16[128,512]{1,0:T(8,128)(2,1)S(1)} %get-tuple-element.23) | copy-start | bytes 393220
  40.5 0.9 copy-start.7
  44.2 10.8 %all-to-all-start.1 = ((bf16[8,16,128]{2,1,0:T(8,128)(2,1)}), bf16[8,16,128]{2,1,0:T(8,128)(2,1)S(1)}, u32[]{:S(2)}, u32[]{:S(2)}) async-start(bf16[8,16,128]{2,1,0:T(8,128)(2,1)} %bitcast.6), calls=%async_computation.1 | async-start | bytes 65536 | tf_op jit(solution)/shard_map/all_to_all | solution.py:147
  55.9 9.1 %copy-start.9 = (f32[128]{0:T(128)}, f32[128]{0:T(128)S(1)}, u32[]{:S(2)}) copy-start(f32[128]{0:T(128)S(1)} %fusion.21) | copy-start | bytes 1540
  56.4 8.6 %copy-start.11 = (f32[128]{0:T(128)}, f32[128]{0:T(128)S(1)}, u32[]{:S(2)}) copy-start(f32[128]{0:T(128)S(1)} %get-tuple-element.18) | copy-start | bytes 1540
  66.3 9.3 %copy-start.13 = (s32[128]{0:T(128)S(1)}, s32[128]{0:T(128)}, u32[]{:S(2)}) copy-start(s32[128]{0:T(128)} %fusion.31) | copy-start | bytes 1540
  66.3 9.3 %all-to-all-start.2 = ((f32[8,16,128]{2,1,0:T(8,128)}), f32[8,16,128]{2,1,0:T(8,128)S(1)}, u32[]{:S(2)}, u32[]{:S(2)}) async-start(f32[8,16,128]{2,1,0:T(8,128)} %bitcast.11), calls=%async_computation.2 | async-start | bytes 131072 | tf_op jit(solution)/shard_map/all_to_all | solution.py:160
  69.8 127.1 %all-reduce.5.cloned.1.call-start = ((), (), s32[]{:S(2)}) async-start(), calls=%async_computation.3 | async-start | bytes 9175040 | tf_op jit(solution)/shard_map/psum | solution.py:173
  94.1 216.9 %all-reduce.7.cloned.1.call-start = ((), (), s32[]{:S(2)}) async-start(), calls=%async_computation.4 | async-start | bytes 9175040 | tf_op jit(solution)/shard_map/psum | solution.py:173
  197.0 0.6 copy-start.10
  197.0 0.6 copy-start.12
  312.6 4.7 %copy-start.4 = (f32[512,128]{1,0:T(8,128)S(1)}, f32[512,128]{1,0:T(8,128)}, u32[]{:S(2)}) copy-start(f32[512,128]{1,0:T(8,128)} %get-tuple-element.37) | copy-start | bytes 786436
Sparse Core Ops, SparseCore 0:
  94.3 102.6 all-reduce.4
  200.8 110.1 all-reduce.6
